TPU v7x, 256 devices: a whole 4x4x8 slice. The times are simulated.
256 devices in a mesh: depth: 2 (over core), lx: 16 (over y, x), ly: 8 (over z).
Axes of the slice: x: 4, y: 4, z: 8, core: 2. Of those that a mesh axis runs over, the one named last changes fastest.
Arguments:
- iterate: float32 [32, 4, 128, 1024], P('depth', None, 'lx', 'ly'), may hold values from -3 to 3
- right_side: float32 [32, 4, 128, 1024], P('depth', None, 'lx', 'ly'), may hold values from -64 to 64
- storage: float32 [32, 128, 1024], P('depth', 'lx', 'ly'), may hold values from 0.02 to 0.2
- zones: int32 [32, 128, 1024], P('depth', 'lx', 'ly'), may hold values from 0 to 7
- counts: int32 [128, 1024], P('lx', 'ly'), may hold values from 8 to 32
- materials: float32 [2, 8, 4, 4], replicated, as said below
Outputs:
- updated: float32 [32, 4, 128, 1024], P('depth', None, 'lx', 'ly')
- coarse: float32 [16, 4, 128, 1024], P('depth', None, 'lx', 'ly')
Inputs may be any that keep to these rules, and one draw needn't show every extreme that they name: Nodes of column (x, y) with depth index below counts[x, y] are active. Each materials[t, k] is a symmetric matrix whose diagonal entries are positive and each larger than the sum of the magnitudes of the other entries in its row.
All inputs are finite; a program needn't handle non-finite values.
Results may differ from a plain program's by a relative error of at most 0.0003.
Values sent between devices are 32-bit elements; how exact they have to be, the bound alone decides.
A program may use at most 64 MiB of HBM per device.

v0:
```python
import jax
import jax.numpy as jnp
from jax import lax
from jax.sharding import PartitionSpec as P


def padded(block, sides, width):
    for axis, dim in sides:
        count = lax.axis_size(axis)
        forward = [(i, i + 1) for i in range(count - 1)]
        backward = [(target, source) for source, target in forward]
        low = lax.ppermute(
            lax.slice_in_dim(block, block.shape[dim] - width, None, axis=dim), axis, forward
        )
        high = lax.ppermute(lax.slice_in_dim(block, 0, width, axis=dim), axis, backward)
        block = jnp.concatenate([low, block, high], axis=dim)
    return block


def shifted(x, axis, by):
    count = lax.axis_size(axis)
    pairs = [(i, i + by) for i in range(count) if 0 <= i + by < count]
    return lax.ppermute(x, axis, pairs)


def box_weights(values):
    values = 0.5 * values[:-2] + values[1:-1] + 0.5 * values[2:]
    values = 0.5 * values[..., :-2, :] + values[..., 1:-1, :] + 0.5 * values[..., 2:, :]
    return 0.5 * values[..., :-2] + values[..., 1:-1] + 0.5 * values[..., 2:]


def inner_part(values):
    return values[1:-1, ..., 1:-1, 1:-1]


def vertical_sum(values):
    return values[2:, ..., 1:-1, 1:-1] + values[:-2, ..., 1:-1, 1:-1]


def lateral_sum(values):
    return box_weights(values) - inner_part(values) - 0.5 * vertical_sum(values)


def lookup_table(weights, table):
    total = weights[0][:, None, None] * table[0][None, :, :, None, None]
    for index in range(1, len(weights)):
        total = total + weights[index][:, None, None] * table[index][None, :, :, None, None]
    return total


def block_apply(matrix, vector):
    total = matrix[..., :, 0, :, :] * vector[..., 0:1, :, :]
    for column in range(1, 4):
        total = total + matrix[..., :, column, :, :] * vector[..., column : column + 1, :, :]
    return total


def block_product(left, right):
    total = left[..., :, 0, :, :][..., :, None, :, :] * right[..., 0, :, :, :][..., None, :, :, :]
    for column in range(1, 4):
        total = (
            total
            + left[..., :, column, :, :][..., :, None, :, :]
            * right[..., column, :, :, :][..., None, :, :, :]
        )
    return total


def block_solve_parts(matrix, right_parts):
    rows = [[matrix[target, column] for column in range(4)] for target in range(4)]
    vectors = [[part[target] for target in range(4)] for part in right_parts]
    for pivot_row in range(4):
        inverse = 1.0 / rows[pivot_row][pivot_row]
        for column in range(pivot_row + 1, 4):
            rows[pivot_row][column] = rows[pivot_row][column] * inverse
        for group in vectors:
            group[pivot_row] = group[pivot_row] * inverse
        for target in range(4):
            if target != pivot_row:
                factor = rows[target][pivot_row]
                for column in range(pivot_row + 1, 4):
                    rows[target][column] = rows[target][column] - factor * rows[pivot_row][column]
                for group in vectors:
                    group[target] = group[target] - factor[None] * group[pivot_row]
    return [jnp.stack(group) for group in vectors]


def coefficients(codes_ext, materials, storage):
    zone_count = materials.shape[1]
    onehots = [(codes_ext == index + 1).astype(jnp.float32) for index in range(zone_count)]
    active_ext = (codes_ext > 0).astype(jnp.float32)
    lat_ext = lookup_table(onehots, materials[0])
    vert_ext = lookup_table(onehots, materials[1])
    lat_counts = [lateral_sum(item) for item in onehots]
    vert_counts = [vertical_sum(item) for item in onehots]
    lat_weight = lateral_sum(active_ext)
    vert_weight = vertical_sum(active_ext)
    active = inner_part(active_ext)
    beside_all = lookup_table(lat_counts, materials[0]) + lookup_table(vert_counts, materials[1])
    identity = jnp.eye(4, dtype=jnp.float32)[None, :, :, None, None]
    diagonal = storage[:, None, None] * identity + 0.5 * active[:, None, None] * (
        inner_part(lat_ext) * lat_weight[:, None, None]
        + inner_part(vert_ext) * vert_weight[:, None, None]
        + beside_all
    )
    column_codes = [item[:, 1:-1, 1:-1] for item in onehots]
    column_active = active_ext[:, 1:-1, 1:-1]
    link = column_active[:-1] * column_active[1:]
    pairs = 0.5 * lookup_table(
        [(item[:-1] + item[1:]) * link for item in column_codes], materials[1]
    )
    return (active, active_ext, lat_ext, vert_ext, diagonal, pairs)


def apply_operator(field_ext, coeffs):
    active, active_ext, lat_ext, vert_ext, diagonal, pairs = coeffs
    gated = field_ext * active_ext[:, None]
    lat_flow = block_apply(lat_ext, field_ext)
    vert_flow = block_apply(vert_ext, field_ext)
    off_part = block_apply(inner_part(lat_ext), lateral_sum(gated)) + lateral_sum(lat_flow)
    off_part = (
        off_part + block_apply(inner_part(vert_ext), vertical_sum(gated)) + vertical_sum(vert_flow)
    )
    return block_apply(diagonal, inner_part(field_ext)) - 0.5 * active[:, None] * off_part


def forward_sweep(diagonal, above, residual, carry_matrix, carry_value):

    def advance(carry, level):
        coupled, carried_value, carried_others = carry
        block, pair, value = level
        parts = [pair, (carried_value + value)[:, None]]
        solved = block_solve_parts(block - coupled, parts)
        gain = solved[0]
        rest_value = solved[1][:, 0]
        rest_others = None
        next_others = None
        next_carry = (block_product(pair, gain), block_apply(pair, rest_value), next_others)
        return (next_carry, (gain, rest_value, rest_others))

    final, stacked = lax.scan(
        advance, (carry_matrix, carry_value, None), (diagonal, above, residual)
    )
    return (stacked[0], stacked[1], stacked[2], final[0], final[1])


def backward_sweep(gains, rest_values, rest_others, start_value):

    def retreat(state, level):
        value_state, others_state, free_state = state
        gain, rest_value, rest_other = level
        value_state = rest_value + block_apply(gain, value_state)
        if others_state is not None:
            others_state = rest_other + block_product(gain, others_state)
            free_state = block_product(gain, free_state)
        state = (value_state, others_state, free_state)
        return (state, state)

    return lax.scan(
        retreat, (start_value, None, None), (gains, rest_values, rest_others), reverse=True
    )[1]


def local(iterate, right_side, storage, zones, counts, materials):
    depth_cells = zones.shape[0]
    plane = zones.shape[1:]
    depth_count = lax.axis_size("depth")
    levels = lax.axis_index("depth") * depth_cells + jnp.arange(depth_cells, dtype=jnp.int32)
    codes = jnp.where(levels[:, None, None] < counts[None], zones + 1, 0)
    joined = jnp.concatenate([iterate, codes.astype(jnp.float32)[:, None]], axis=1)
    joined_ext = padded(joined, (("depth", 0), ("lx", 2), ("ly", 3)), 1)
    field_ext = joined_ext[:, :4]
    codes_ext = joined_ext[:, 4].astype(jnp.int32)
    coeffs = coefficients(codes_ext, materials, storage)
    active, active_ext, lat_ext, vert_ext, diagonal, pairs = coeffs
    residual = active[:, None] * (right_side - apply_operator(field_ext, coeffs))
    above = pairs[1:]
    zero_matrix = jnp.zeros((4, 4) + plane, jnp.float32)
    zero_vector = jnp.zeros((4,) + plane, jnp.float32)
    coupled = zero_matrix
    carried = zero_vector
    for round_index in range(depth_count):
        if round_index > 0:
            coupled, carried = shifted((outgoing_matrix, outgoing_vector), "depth", 1)
        gains, rest_values, rest_others, outgoing_matrix, outgoing_vector = forward_sweep(
            diagonal, above, residual, coupled, carried
        )
    incoming = zero_vector
    for round_index in range(depth_count):
        if round_index > 0:
            incoming = shifted(first_value, "depth", -1)
        value_states = backward_sweep(gains, rest_values, rest_others, incoming)[0]
        first_value = value_states[0]
    updated = iterate + value_states
    correction_ext = padded(value_states, (("depth", 0), ("lx", 2), ("ly", 3)), 1)
    smoothed = residual - apply_operator(correction_ext, coeffs)
    below_plane = shifted(smoothed[-1], "depth", 1)
    paired = smoothed.reshape((depth_cells // 2, 2) + smoothed.shape[1:])
    even_planes = paired[:, 0]
    odd_planes = paired[:, 1]
    previous = jnp.concatenate([below_plane[None], odd_planes[:-1]], axis=0)
    coarse = 0.5 * previous + even_planes + 0.5 * odd_planes
    return (updated, coarse)


def solution(mesh):
    placed = (
        P("depth", None, "lx", "ly"),
        P("depth", None, "lx", "ly"),
        P("depth", "lx", "ly"),
        P("depth", "lx", "ly"),
        P("lx", "ly"),
        P(),
    )
    return jax.shard_map(
        local,
        mesh=mesh,
        in_specs=placed,
        out_specs=(P("depth", None, "lx", "ly"), P("depth", None, "lx", "ly")),
        check_vma=False,
    )
```

profile of v0, /device:TPU:153, one launch (start us, length us, event | category | flops | bytes accessed | tf_op | source)
XLA Modules:
  0.0 178.0 jit_solution(12796506499672215517)
XLA Ops:
  2.4 2.6 %collective-permute-start.1 = (f32[1,5,8,128]{3,2,1,0:T(8,128)S(1)}, f32[1,5,8,128]{3,2,1,0:T(8,128)S(1)}, u32[]{:S(2)}, u32[]{:S(2)}) collective-permute-start(f32[1,5,8,128]{3,2,1,0:T(8,128)S(1)} %get-tuple-element.633), channel_id=1, source_target_pairs={{128,0},{129,1},{130,2},{131,3},{132,4},{133,5},{134,6},{135,7},{1... | collective-permute-start | bytes 61448 | tf_op jit(solution)/shard_map/ppermute | solution.py:15
  5.0 1.3 collective-permute-start
  6.3 1.6 slice_bitcast_fusion.75
  8.1 4.6 %collective-permute-start.3 = (f32[18,5,1,128]{3,2,1,0:T(1,128)S(1)}, f32[18,5,1,128]{3,2,1,0:T(1,128)S(1)}, u32[]{:S(2)}, u32[]{:S(2)}) collective-permute-start(f32[18,5,1,128]{3,2,1,0:T(1,128)S(1)} %get-tuple-element.631), channel_id=1, source_target_pairs={{8,0},{16,8},{24,16},{32,24},{40,32},{48,40},{56,48},{64,56},{72,6... | collective-permute-start | bytes 138248 | tf_op jit(solution)/shard_map/ppermute | solution.py:15
  12.7 1.9 %collective-permute-start.2 = (f32[18,5,1,128]{3,2,1,0:T(1,128)S(1)}, f32[18,5,1,128]{3,2,1,0:T(1,128)S(1)}, u32[]{:S(2)}, u32[]{:S(2)}) collective-permute-start(f32[18,5,1,128]{3,2,1,0:T(1,128)S(1)} %get-tuple-element.630), channel_id=1, source_target_pairs={{0,8},{8,16},{16,24},{24,32},{32,40},{40,48},{48,56},{56,64},{64,7... | collective-permute-start | bytes 138248 | tf_op jit(solution)/shard_map/ppermute | solution.py:12
  14.9 4.7 %collective-permute-done.2 = f32[18,5,1,128]{3,2,1,0:T(1,128)S(1)} collective-permute-done((f32[18,5,1,128]{3,2,1,0:T(1,128)S(1)}, f32[18,5,1,128]{3,2,1,0:T(1,128)S(1)}, u32[]{:S(2)}, u32[]{:S(2)}) %collective-permute-start.2) | collective-permute-done | bytes 46112 | tf_op jit(solution)/shard_map/ppermute | solution.py:12
  20.4 1.9 %collective-permute-start.5 = (f32[18,5,10,1]{0,3,2,1:T(1,128)S(1)}, f32[18,5,10,1]{0,3,2,1:T(1,128)S(1)}, u32[]{:S(2)}, u32[]{:S(2)}) collective-permute-start(f32[18,5,10,1]{0,3,2,1:T(1,128)S(1)} %copy.125), channel_id=1, source_target_pairs={{1,0},{2,1},{3,2},{4,3},{5,4},{6,5},{7,6},{9,8},{10,9},{11,10},{12... | collective-permute-start | bytes 10808 | tf_op jit(solution)/shard_map/ppermute | solution.py:15
  22.7 3.4 %collective-permute-start.4 = (f32[18,5,10,1]{0,3,2,1:T(1,128)S(1)}, f32[18,5,10,1]{0,3,2,1:T(1,128)S(1)}, u32[]{:S(2)}, u32[]{:S(2)}) collective-permute-start(f32[18,5,10,1]{0,3,2,1:T(1,128)S(1)} %copy.124), channel_id=1, source_target_pairs={{0,1},{1,2},{2,3},{3,4},{4,5},{5,6},{6,7},{8,9},{9,10},{10,11},{11... | collective-permute-start | bytes 10808 | tf_op jit(solution)/shard_map/ppermute | solution.py:12
  34.2 2.4 %multiply_add_fusion.4 = f32[18,4,4,10,130]{4,3,1,0,2:T(8,128)S(1)} fusion(f32[4,4]{0,1:T(4,128)S(1)} %copy.151, f32[4,4]{0,1:T(4,128)S(1)} %copy.150, f32[4,4]{0,1:T(4,128)S(1)} %copy.149, f32[4,4]{0,1:T(4,128)S(1)} %copy.148, f32[4,4]{0,1:T(4,128)S(1)} %copy.147, f32[4,4]{0,1:T(4,128)S(1)} %copy.146, f32[4,4]{0,1:T(4,128)S(1)} %copy.145, ...), kind=kLoop, calls=%fused_computation.271 | loop fusion | flops 5616000 | bytes 2246912 | tf_op jit(solution)/shard_map/add | solution.py:47
  36.6 2.4 %multiply_add_fusion.5 = f32[18,4,4,10,130]{4,3,1,0,2:T(8,128)S(1)} fusion(f32[4,4]{0,1:T(4,128)S(1)} %bitcast.1214, f32[18,10,130]{2,1,0:T(8,128)S(1)} %get-tuple-element.616, f32[4,4]{0,1:T(4,128)S(1)} %bitcast.1216, f32[18,10,130]{2,1,0:T(8,128)S(1)} %get-tuple-element.607, f32[4,4]{0,1:T(4,128)S(1)} %bitcast.1218, ...), kind=kLoop, calls=%fused_computation.272 | loop fusion | flops 5616000 | bytes 2246912 | tf_op jit(solution)/shard_map/add | solution.py:47
  39.0 2.4 %fusion.108 = f32[16,4,4,8,128]{4,3,1,0,2:T(8,128)S(1)} fusion(f32[18,4,4,10,130]{4,3,1,0,2:T(8,128)S(1)} %multiply_add_fusion.4, f32[18,4,4,10,130]{4,3,1,0,2:T(8,128)S(1)} %multiply_add_fusion.5, f32[4,4]{0,1:T(4,128)S(1)} %copy.151, f32[16,8,128]{2,1,0:T(8,128)S(1)} %get-tuple-element.538, f32[4,4]{0,1:T(4,128)S(1)} %copy.150, ...), kind=kLoop, calls=%fused_computation.309 | loop fusion | flops 9961472 | bytes 4457536 | tf_op jit(solution)/shard_map/add | solution.py:101
  42.6 1.6 multiply_add_fusion.9
  48.3 18.8 %while.64 = (s32[]{:T(128)}, f32[4,4,8,128]{3,2,1,0:T(8,128)S(1)}, f32[4,8,128]{2,1,0:T(8,128)S(1)}, f32[16,4,4,8,128]{4,3,2,1,0:T(8,128)S(1)}, f32[16,4,4,8,128...) while((s32[]{:T(128)}, f32[4,4,8,128]{3,2,1,0:T(8,128)S(1)}, ...), condition=%wide.region_1.2_spmd.clone, body=%wide.region_0.1_spmd.clone.sunk | while | flops 430086 | bytes 1487040 | solution.py:141
  67.1 1.3 collective-permute-start.6
  68.4 1.3 collective-permute-start.7
  69.8 3.9 %collective-permute-done.7 = f32[4,8,128]{2,1,0:T(8,128)S(1)} collective-permute-done((f32[4,8,128]{2,1,0:T(8,128)S(1)}, f32[4,8,128]{2,1,0:T(8,128)S(1)}, u32[]{:S(2)}, u32[]{:S(2)}) %collective-permute-start.7) | collective-permute-done | bytes 16416 | tf_op jit(solution)/shard_map/ppermute | solution.py:23
  73.7 29.7 %while.62 = (s32[]{:T(128)}, f32[4,4,8,128]{3,2,1,0:T(8,128)S(1)}, f32[4,8,128]{2,1,0:T(8,128)S(1)}, f32[16,4,4,8,128]{4,3,1,2,0:T(8,128)}, f32[16,4,8,128]{3,2,...) while((s32[]{:T(128)}, f32[4,4,8,128]{3,2,1,0:T(8,128)S(1)}, ...), condition=%wide.region_3.4_spmd, body=%wide.region_2.3_spmd.sunk | while | flops 593925 | bytes 1954013 | solution.py:141
  103.4 14.9 %while.65 = (s32[]{:T(128)}, f32[4,8,128]{2,1,0:T(8,128)S(1)}, f32[16,4,8,128]{3,2,1,0:T(8,128)S(1)}, f32[16,4,8,128]{3,2,1,0:T(8,128)S(1)}, f32[16,4,4,8,128]{4...) while((s32[]{:T(128)}, f32[4,8,128]{2,1,0:T(8,128)S(1)}, f32[16,4,8,128]{3,2,1,0:T(8,128)S(1)}, ...), condition=%wide.region_5.6_spmd.clone, body=%wide.region_4.5_spmd.clone.sunk | while | flops 69636 | bytes 426111 | solution.py:159
  118.3 2.1 %collective-permute-start.8 = (f32[4,8,128]{2,1,0:T(8,128)S(1)}, f32[4,8,128]{2,1,0:T(8,128)S(1)}, u32[]{:S(2)}, u32[]{:S(2)}) collective-permute-start(f32[4,8,128]{2,1,0:T(8,128)S(1)} %slice_bitcast_fusion.77), channel_id=1, source_target_pairs={{128,0},{129,1},{130,2},{131,3},{132,4},{133,5},{134,6},{135,7},{1... | collective-permute-start | bytes 49160 | tf_op jit(solution)/shard_map/ppermute | solution.py:23
  121.2 14.4 %while.63 = (s32[]{:T(128)}, f32[4,8,128]{2,1,0:T(8,128)S(1)}, f32[16,4,8,128]{3,2,1,0:T(8,128)S(1)}, f32[16,4,8,128]{3,2,1,0:T(8,128)S(1)}, f32[16,4,4,8,128]{4,3,1,2,0:T(8,128)}, /*index=5*/s32[]{:T(128)}, s32[]{:T(128)}) while((s32[]{:T(128)}, f32[4,8,128]{2,1,0:T(8,128)S(1)}, f32[16,4,8,128]{3,2,1,0:T(8,128)S(1)}, ...), condition=%wide.region_7.8_spmd, body=%wide.region_6.7_spmd.sunk | while | flops 65539 | bytes 393325 | solution.py:159
  135.7 1.3 collective-permute-start.9
  137.0 3.0 %collective-permute-start.10 = (f32[1,4,8,128]{3,2,1,0:T(8,128)S(1)}, f32[1,4,8,128]{3,2,1,0:T(8,128)S(1)}, u32[]{:S(2)}, u32[]{:S(2)}) collective-permute-start(f32[1,4,8,128]{3,2,1,0:T(8,128)S(1)} %get-tuple-element.650), channel_id=1, source_target_pairs={{128,0},{129,1},{130,2},{131,3},{132,4},{133,5},{134,6},{135,7},{1... | collective-permute-start | bytes 49160 | tf_op jit(solution)/shard_map/ppermute | solution.py:15
  140.9 1.9 %collective-permute-start.12 = (f32[18,4,1,128]{3,2,1,0:T(1,128)S(1)}, f32[18,4,1,128]{3,2,1,0:T(1,128)S(1)}, u32[]{:S(2)}, u32[]{:S(2)}) collective-permute-start(f32[18,4,1,128]{3,2,1,0:T(1,128)S(1)} %get-tuple-element.635), channel_id=1, source_target_pairs={{8,0},{16,8},{24,16},{32,24},{40,32},{48,40},{56,48},{64,56},{72,6... | collective-permute-start | bytes 110600 | tf_op jit(solution)/shard_map/ppermute | solution.py:15
  142.8 3.4 %collective-permute-start.11 = (f32[18,4,1,128]{3,2,1,0:T(1,128)S(1)}, f32[18,4,1,128]{3,2,1,0:T(1,128)S(1)}, u32[]{:S(2)}, u32[]{:S(2)}) collective-permute-start(f32[18,4,1,128]{3,2,1,0:T(1,128)S(1)} %get-tuple-element.634), channel_id=1, source_target_pairs={{0,8},{8,16},{16,24},{24,32},{32,40},{40,48},{48,56},{56,64},{64,7... | collective-permute-start | bytes 110600 | tf_op jit(solution)/shard_map/ppermute | solution.py:12
  146.2 3.4 %collective-permute-done.11 = f32[18,4,1,128]{3,2,1,0:T(1,128)S(1)} collective-permute-done((f32[18,4,1,128]{3,2,1,0:T(1,128)S(1)}, f32[18,4,1,128]{3,2,1,0:T(1,128)S(1)}, u32[]{:S(2)}, u32[]{:S(2)}) %collective-permute-start.11) | collective-permute-done | bytes 36896 | tf_op jit(solution)/shard_map/ppermute | solution.py:12
  150.3 2.8 %collective-permute-start.14 = (f32[18,4,10,1]{0,1,3,2:T(4,128)S(1)}, f32[18,4,10,1]{0,1,3,2:T(4,128)S(1)}, u32[]{:S(2)}, u32[]{:S(2)}) collective-permute-start(f32[18,4,10,1]{0,1,3,2:T(4,128)S(1)} %copy.177), channel_id=1, source_target_pairs={{1,0},{2,1},{3,2},{4,3},{5,4},{6,5},{7,6},{9,8},{10,9},{11,10},{12... | collective-permute-start | bytes 8648 | tf_op jit(solution)/shard_map/ppermute | solution.py:15
  153.5 2.9 %collective-permute-start.13 = (f32[18,4,10,1]{0,1,3,2:T(4,128)S(1)}, f32[18,4,10,1]{0,1,3,2:T(4,128)S(1)}, u32[]{:S(2)}, u32[]{:S(2)}) collective-permute-start(f32[18,4,10,1]{0,1,3,2:T(4,128)S(1)} %copy.176), channel_id=1, source_target_pairs={{0,1},{1,2},{2,3},{3,4},{4,5},{5,6},{6,7},{8,9},{9,10},{10,11},{11... | collective-permute-start | bytes 8648 | tf_op jit(solution)/shard_map/ppermute | solution.py:12
  157.8 1.4 collective-permute-done.13
  160.9 5.3 %multiply_add_fusion.7 = (f32[18,4,10,130]{3,2,1,0:T(8,128)S(1)}, f32[18,4,10,130]{3,2,1,0:T(8,128)S(1)}) fusion(f32[18,4,4,10,130]{4,3,1,0,2:T(8,128)} %copy-done.1, f32[18,10,130]{2,1,0:T(8,128)S(1)} %get-tuple-element.623, f32[18,10,130]{2,1,0:T(8,128)S(1)} %get-tuple-element.621, f32[18,10,130]{2,1,0:T(8,128)S(1)} %get-tuple-element.622, ...), kind=kLoop, calls=%fused_computation.285 | loop fusion | flops 1310400 | bytes 4118400 | tf_op jit(solution)/shard_map/add | solution.py:54
  167.7 4.7 %fusion.129 = f32[16,4,8,128]{3,2,1,0:T(8,128)S(1)} fusion(f32[16,4,8,128]{3,2,1,0:T(8,128)S(1)} %get-tuple-element.1173, f32[18,4,10,130]{3,2,1,0:T(8,128)S(1)} %get-tuple-element.619, f32[18,4,10,130]{3,2,1,0:T(8,128)S(1)} %get-tuple-element.618, f32[16,4,8,130]{3,2,1,0:T(8,128)S(1)} %fusion.114, f32[16,4,4,8,128]{4,3,1,0,2:T(8,128)S(1)} %fusion.108, ...), kind=kLoop, calls=%fused_computation.367 | loop fusion | flops 2359296 | bytes 6619136 | tf_op jit(solution)/shard_map/sub | solution.py:196
  172.4 1.3 collective-permute-start.15
  173.7 3.6 %collective-permute-done.15 = f32[4,8,128]{2,1,0:T(8,128)S(1)} collective-permute-done((f32[4,8,128]{2,1,0:T(8,128)S(1)}, f32[4,8,128]{2,1,0:T(8,128)S(1)}, u32[]{:S(2)}, u32[]{:S(2)}) %collective-permute-start.15) | collective-permute-done | bytes 16416 | tf_op jit(solution)/shard_map/ppermute | solution.py:23
  (849 shorter events, 97.7 us)
Async XLA Ops:
  0.6 7.4 %copy-start.2 = (f32[16,4,8,128]{3,2,1,0:T(8,128)S(1)}, f32[16,4,8,128]{3,2,1,0:T(8,128)}, u32[]{:S(2)}) copy-start(f32[16,4,8,128]{3,2,1,0:T(8,128)} %param.14) | copy-start | bytes 786436
  0.6 14.0 %copy-start.5 = (f32[2,8,4,4]{1,3,2,0:T(4,128)S(1)}, f32[2,8,4,4]{1,3,2,0:T(4,128)}, u32[]{:S(2)}) copy-start(f32[2,8,4,4]{1,3,2,0:T(4,128)} %param.19) | copy-start | bytes 3076
  2.4 5.5 %collective-permute-start.1 = (f32[1,5,8,128]{3,2,1,0:T(8,128)S(1)}, f32[1,5,8,128]{3,2,1,0:T(8,128)S(1)}, u32[]{:S(2)}, u32[]{:S(2)}) collective-permute-start(f32[1,5,8,128]{3,2,1,0:T(8,128)S(1)} %get-tuple-element.633), channel_id=1, source_target_pairs={{128,0},{129,1},{130,2},{131,3},{132,4},{133,5},{134,6},{135,7},{1... | collective-permute-start | bytes 61448 | tf_op jit(solution)/shard_map/ppermute | solution.py:15
  5.0 3.1 %collective-permute-start = (f32[1,5,8,128]{3,2,1,0:T(8,128)S(1)}, f32[1,5,8,128]{3,2,1,0:T(8,128)S(1)}, u32[]{:S(2)}, u32[]{:S(2)}) collective-permute-start(f32[1,5,8,128]{3,2,1,0:T(8,128)S(1)} %get-tuple-element.632), channel_id=1, source_target_pairs={{0,128},{1,129},{2,130},{3,131},{4,132},{5,133},{6,134},{7,135},{8... | collective-permute-start | bytes 61448 | tf_op jit(solution)/shard_map/ppermute | solution.py:12
  8.1 6.8 %collective-permute-start.3 = (f32[18,5,1,128]{3,2,1,0:T(1,128)S(1)}, f32[18,5,1,128]{3,2,1,0:T(1,128)S(1)}, u32[]{:S(2)}, u32[]{:S(2)}) collective-permute-start(f32[18,5,1,128]{3,2,1,0:T(1,128)S(1)} %get-tuple-element.631), channel_id=1, source_target_pairs={{8,0},{16,8},{24,16},{32,24},{40,32},{48,40},{56,48},{64,56},{72,6... | collective-permute-start | bytes 138248 | tf_op jit(solution)/shard_map/ppermute | solution.py:15
  12.7 6.9 %collective-permute-start.2 = (f32[18,5,1,128]{3,2,1,0:T(1,128)S(1)}, f32[18,5,1,128]{3,2,1,0:T(1,128)S(1)}, u32[]{:S(2)}, u32[]{:S(2)}) collective-permute-start(f32[18,5,1,128]{3,2,1,0:T(1,128)S(1)} %get-tuple-element.630), channel_id=1, source_target_pairs={{0,8},{8,16},{16,24},{24,32},{32,40},{40,48},{48,56},{56,64},{64,7... | collective-permute-start | bytes 138248 | tf_op jit(solution)/shard_map/ppermute | solution.py:12
  14.8 11.8 %copy-start.18 = (f32[4,4]{1,0:T(4,128)}, f32[4,4]{1,0:T(4,128)S(1)}, u32[]{:S(2)}) copy-start(f32[4,4]{1,0:T(4,128)S(1)} %get-tuple-element.682) | copy-start | bytes 196
  14.8 11.9 %copy-start.16 = (f32[4,4]{1,0:T(4,128)}, f32[4,4]{1,0:T(4,128)S(1)}, u32[]{:S(2)}) copy-start(f32[4,4]{1,0:T(4,128)S(1)} %get-tuple-element.681) | copy-start | bytes 196
  14.9 12.0 %copy-start.14 = (f32[4,4]{1,0:T(4,128)}, f32[4,4]{1,0:T(4,128)S(1)}, u32[]{:S(2)}) copy-start(f32[4,4]{1,0:T(4,128)S(1)} %get-tuple-element.680) | copy-start | bytes 196
  14.9 12.1 %copy-start.20 = (f32[4,4]{1,0:T(4,128)}, f32[4,4]{1,0:T(4,128)S(1)}, u32[]{:S(2)}) copy-start(f32[4,4]{1,0:T(4,128)S(1)} %get-tuple-element.683) | copy-start | bytes 196
  20.4 7.9 %collective-permute-start.5 = (f32[18,5,10,1]{0,3,2,1:T(1,128)S(1)}, f32[18,5,10,1]{0,3,2,1:T(1,128)S(1)}, u32[]{:S(2)}, u32[]{:S(2)}) collective-permute-start(f32[18,5,10,1]{0,3,2,1:T(1,128)S(1)} %copy.125), channel_id=1, source_target_pairs={{1,0},{2,1},{3,2},{4,3},{5,4},{6,5},{7,6},{9,8},{10,9},{11,10},{12... | collective-permute-start | bytes 10808 | tf_op jit(solution)/shard_map/ppermute | solution.py:15
  22.7 6.1 %collective-permute-start.4 = (f32[18,5,10,1]{0,3,2,1:T(1,128)S(1)}, f32[18,5,10,1]{0,3,2,1:T(1,128)S(1)}, u32[]{:S(2)}, u32[]{:S(2)}) collective-permute-start(f32[18,5,10,1]{0,3,2,1:T(1,128)S(1)} %copy.124), channel_id=1, source_target_pairs={{0,1},{1,2},{2,3},{3,4},{4,5},{5,6},{6,7},{8,9},{9,10},{10,11},{11... | collective-permute-start | bytes 10808 | tf_op jit(solution)/shard_map/ppermute | solution.py:12
  36.6 10.1 %copy-start = (f32[18,4,4,10,130]{4,3,1,0,2:T(8,128)}, f32[18,4,4,10,130]{4,3,1,0,2:T(8,128)S(1)}, u32[]{:S(2)}) copy-start(f32[18,4,4,10,130]{4,3,1,0,2:T(8,128)S(1)} %multiply_add_fusion.4) | copy-start | bytes 4492804
  36.6 2.4 %copy-start.13 = (f32[16,8,128]{2,1,0:T(8,128)S(1)}, f32[16,8,128]{2,1,0:T(8,128)}, u32[]{:S(2)}) copy-start(f32[16,8,128]{2,1,0:T(8,128)} %param.16) | copy-start | bytes 196612
  36.6 2.4 %copy-start.22 = (f32[4,4]{0,1:T(4,128)S(1)}, f32[4,4]{0,1:T(4,128)}, u32[]{:S(2)}) copy-start(f32[4,4]{0,1:T(4,128)} %fusion.207) | copy-start | bytes 196
  39.0 7.7 %copy-start.1 = (f32[18,4,4,10,130]{4,3,1,0,2:T(8,128)}, f32[18,4,4,10,130]{4,3,1,0,2:T(8,128)S(1)}, u32[]{:S(2)}) copy-start(f32[18,4,4,10,130]{4,3,1,0,2:T(8,128)S(1)} %multiply_add_fusion.5) | copy-start | bytes 4492804
  46.0 0.9 copy-start.7
  46.0 0.9 copy-start.8
  46.0 1.0 copy-start.12
  67.1 6.5 %collective-permute-start.6 = (f32[4,4,8,128]{3,2,1,0:T(8,128)S(1)}, f32[4,4,8,128]{3,2,1,0:T(8,128)S(1)}, u32[]{:S(2)}, u32[]{:S(2)}) collective-permute-start(f32[4,4,8,128]{3,2,1,0:T(8,128)S(1)} %get-tuple-element.284), channel_id=1, source_target_pairs={{0,128},{1,129},{2,130},{3,131},{4,132},{5,133},{6,134},{7,135},{8... | collective-permute-start | bytes 196616 | tf_op jit(solution)/shard_map/ppermute | solution.py:23
  68.4 5.2 %collective-permute-start.7 = (f32[4,8,128]{2,1,0:T(8,128)S(1)}, f32[4,8,128]{2,1,0:T(8,128)S(1)}, u32[]{:S(2)}, u32[]{:S(2)}) collective-permute-start(f32[4,8,128]{2,1,0:T(8,128)S(1)} %get-tuple-element.285), channel_id=1, source_target_pairs={{0,128},{1,129},{2,130},{3,131},{4,132},{5,133},{6,134},{7,135},{8... | collective-permute-start | bytes 49160 | tf_op jit(solution)/shard_map/ppermute | solution.py:23
  118.3 2.9 %collective-permute-start.8 = (f32[4,8,128]{2,1,0:T(8,128)S(1)}, f32[4,8,128]{2,1,0:T(8,128)S(1)}, u32[]{:S(2)}, u32[]{:S(2)}) collective-permute-start(f32[4,8,128]{2,1,0:T(8,128)S(1)} %slice_bitcast_fusion.77), channel_id=1, source_target_pairs={{128,0},{129,1},{130,2},{131,3},{132,4},{133,5},{134,6},{135,7},{1... | collective-permute-start | bytes 49160 | tf_op jit(solution)/shard_map/ppermute | solution.py:23
  135.7 4.3 %collective-permute-start.9 = (f32[1,4,8,128]{3,2,1,0:T(8,128)S(1)}, f32[1,4,8,128]{3,2,1,0:T(8,128)S(1)}, u32[]{:S(2)}, u32[]{:S(2)}) collective-permute-start(f32[1,4,8,128]{3,2,1,0:T(8,128)S(1)} %get-tuple-element.651), channel_id=1, source_target_pairs={{0,128},{1,129},{2,130},{3,131},{4,132},{5,133},{6,134},{7,135},{8... | collective-permute-start | bytes 49160 | tf_op jit(solution)/shard_map/ppermute | solution.py:12
  137.0 3.9 %collective-permute-start.10 = (f32[1,4,8,128]{3,2,1,0:T(8,128)S(1)}, f32[1,4,8,128]{3,2,1,0:T(8,128)S(1)}, u32[]{:S(2)}, u32[]{:S(2)}) collective-permute-start(f32[1,4,8,128]{3,2,1,0:T(8,128)S(1)} %get-tuple-element.650), channel_id=1, source_target_pairs={{128,0},{129,1},{130,2},{131,3},{132,4},{133,5},{134,6},{135,7},{1... | collective-permute-start | bytes 49160 | tf_op jit(solution)/shard_map/ppermute | solution.py:15
  140.8 8.8 %copy-start.3 = (f32[18,4,8,128]{3,2,1,0:T(8,128)}, f32[18,4,8,128]{3,2,1,0:T(8,128)S(1)}, u32[]{:S(2)}) copy-start(f32[18,4,8,128]{3,2,1,0:T(8,128)S(1)} %constant_dynamic-update-slice_fusion) | copy-start | bytes 884740
  140.9 5.3 %collective-permute-start.12 = (f32[18,4,1,128]{3,2,1,0:T(1,128)S(1)}, f32[18,4,1,128]{3,2,1,0:T(1,128)S(1)}, u32[]{:S(2)}, u32[]{:S(2)}) collective-permute-start(f32[18,4,1,128]{3,2,1,0:T(1,128)S(1)} %get-tuple-element.635), channel_id=1, source_target_pairs={{8,0},{16,8},{24,16},{32,24},{40,32},{48,40},{56,48},{64,56},{72,6... | collective-permute-start | bytes 110600 | tf_op jit(solution)/shard_map/ppermute | solution.py:15
  142.8 6.8 %collective-permute-start.11 = (f32[18,4,1,128]{3,2,1,0:T(1,128)S(1)}, f32[18,4,1,128]{3,2,1,0:T(1,128)S(1)}, u32[]{:S(2)}, u32[]{:S(2)}) collective-permute-start(f32[18,4,1,128]{3,2,1,0:T(1,128)S(1)} %get-tuple-element.634), channel_id=1, source_target_pairs={{0,8},{8,16},{16,24},{24,32},{32,40},{40,48},{48,56},{56,64},{64,7... | collective-permute-start | bytes 110600 | tf_op jit(solution)/shard_map/ppermute | solution.py:12
  150.3 9.6 %copy-start.4 = (f32[18,4,8,128]{3,2,1,0:T(8,128)S(1)}, f32[18,4,8,128]{3,2,1,0:T(8,128)}, u32[]{:S(2)}) copy-start(f32[18,4,8,128]{3,2,1,0:T(8,128)} %copy-done.3) | copy-start | bytes 884740
  150.3 6.7 %collective-permute-start.14 = (f32[18,4,10,1]{0,1,3,2:T(4,128)S(1)}, f32[18,4,10,1]{0,1,3,2:T(4,128)S(1)}, u32[]{:S(2)}, u32[]{:S(2)}) collective-permute-start(f32[18,4,10,1]{0,1,3,2:T(4,128)S(1)} %copy.177), channel_id=1, source_target_pairs={{1,0},{2,1},{3,2},{4,3},{5,4},{6,5},{7,6},{9,8},{10,9},{11,10},{12... | collective-permute-start | bytes 8648 | tf_op jit(solution)/shard_map/ppermute | solution.py:15
  153.5 5.7 %collective-permute-start.13 = (f32[18,4,10,1]{0,1,3,2:T(4,128)S(1)}, f32[18,4,10,1]{0,1,3,2:T(4,128)S(1)}, u32[]{:S(2)}, u32[]{:S(2)}) collective-permute-start(f32[18,4,10,1]{0,1,3,2:T(4,128)S(1)} %copy.176), channel_id=1, source_target_pairs={{0,1},{1,2},{2,3},{3,4},{4,5},{5,6},{6,7},{8,9},{9,10},{10,11},{11... | collective-permute-start | bytes 8648 | tf_op jit(solution)/shard_map/ppermute | solution.py:12
  166.8 0.9 copy-start.11
  172.4 4.9 %collective-permute-start.15 = (f32[4,8,128]{2,1,0:T(8,128)S(1)}, f32[4,8,128]{2,1,0:T(8,128)S(1)}, u32[]{:S(2)}, u32[]{:S(2)}) collective-permute-start(f32[4,8,128]{2,1,0:T(8,128)S(1)} %slice_bitcast_fusion.76), channel_id=1, source_target_pairs={{0,128},{1,129},{2,130},{3,131},{4,132},{5,133},{6,134},{7,135},{8... | collective-permute-start | bytes 49160 | tf_op jit(solution)/shard_map/ppermute | solution.py:23
  (7 other events, 5.3 us)
where the time goes:
time: 182 us; the launch traced here: 178 us
  other arithmetic  77.5 us (43%)
  local copies, waits for them, and re-layouts  39.5 us (22%)
  starting transfers between devices  36.8 us (20%)
  waiting for transfers between devices  18.1 us (10%)
  loops' own time  4.51 us (2%)
    squeeze x64, local copies, waits for them, and re-layouts, forward_sweep(): lax.scan(advance, (carry_matrix, carry_value, None), (diagonal, above, re...  27.6 us
    sub x32, other arithmetic, advance(): solved = block_solve_parts(block - coupled, parts)  27.3 us
    ppermute x6, starting transfers between devices, padded(): lax.ppermute(lax.slice_in_dim(block, 0, width, axis=dim), axis, backward)  16.8 us
    ppermute x6, starting transfers between devices, padded(): lax.ppermute(lax.slice_in_dim(block, block.shape[dim] - width, None, axis...  14.1 us
    dynamic_update_slice x64, other arithmetic, forward_sweep(): lax.scan(advance, (carry_matrix, carry_value, None), (diagonal, above, re...  10.6 us
    ppermute x6, waiting for transfers between devices, padded(): lax.ppermute(lax.slice_in_dim(block, block.shape[dim] - width, None, axis...  9.75 us
    ppermute x4, waiting for transfers between devices, shifted(): return lax.ppermute(x, axis, pairs)  8.29 us
    add x34, other arithmetic, block_apply(): total + matrix[..., :, column, :, :] * vector[..., column:column + 1, :, :]  7.28 us
  transfers between devices with their start and end apart: 16, of which 8 were waited for; matrix products, arithmetic and copies ran while one was open for 4% of the time, Pallas kernels for 0%

commit v1 on v0

v1 whole, which is shorter than its diff:
```python
import functools

import jax
import jax.numpy as jnp
from jax import lax
from jax.experimental import pallas as pl
from jax.experimental.pallas import tpu as pltpu
from jax.sharding import PartitionSpec as P

F32 = jnp.float32
MESH = pl.DeviceIdType.MESH
Z = 16
SYM = [(i, j) for i in range(4) for j in range(i, 4)]
AT = {}
for _n, (_i, _j) in enumerate(SYM):
    AT[_i, _j] = _n
    AT[_j, _i] = _n


def sym_apply(m, v):
    out = []
    for i in range(4):
        a = m[AT[i, 0]] * v[0] + m[AT[i, 1]] * v[1]
        b = m[AT[i, 2]] * v[2] + m[AT[i, 3]] * v[3]
        out.append(a + b)
    return out


def sym_inverse(s, sa):
    def small(a, b, c, ra, rc):
        ca, cc = a * ra, c * rc
        q = 1.0 / (ca * cc - (b * ra) * (b * rc))
        return (cc * ra) * q, -((b * ra) * rc) * q, (ca * rc) * q

    a00, a01, a11 = small(s[AT[0, 0]], s[AT[0, 1]], s[AT[1, 1]], sa[0], sa[1])
    s02, s03, s12, s13 = s[AT[0, 2]], s[AT[0, 3]], s[AT[1, 2]], s[AT[1, 3]]
    e00, e01 = a00 * s02 + a01 * s12, a00 * s03 + a01 * s13
    e10, e11 = a01 * s02 + a11 * s12, a01 * s03 + a11 * s13
    c00 = s[AT[2, 2]] - (s02 * e00 + s12 * e10)
    c01 = s[AT[2, 3]] - (s02 * e01 + s12 * e11)
    c11 = s[AT[3, 3]] - (s03 * e01 + s13 * e11)
    x22, x23, x33 = small(c00, c01, c11, sa[2], sa[3])
    x02, x03 = -(e00 * x22 + e01 * x23), -(e00 * x23 + e01 * x33)
    x12, x13 = -(e10 * x22 + e11 * x23), -(e10 * x23 + e11 * x33)
    x00 = a00 - (x02 * e00 + x03 * e01)
    x01 = a01 - (x02 * e10 + x03 * e11)
    x11 = a11 - (x12 * e10 + x13 * e11)
    return [x00, x01, x02, x03, x11, x12, x13, x22, x23, x33]


def kernel(
    sizes,
    it_hbm, rhs_hbm, st_hbm, zn_hbm, ct_hbm, mat_hbm,
    up_hbm, co_hbm,
    mat, fi, rh, st, zn, ct, tab, cd, kl, mv, lk, gf, cf, up, sm, cu,
    inv, gain, sc, bv, rest,
    pk, sxc, sxi, sxd,
    rxc, rxi, rxd, ryc, ryi, ryd, rcc, rci, rcd,
    klx, kly, gx, gt, xt, yt,
    ifm_s, ifm_r, ifv_s, ifv_r, sm_r,
    ld_sem, out_sem, send, recv,
):
    n_lx, n_ly = sizes
    d = lax.axis_index("depth")
    x = lax.axis_index("lx")
    y = lax.axis_index("ly")
    o = 1 - d

    def near(dp, sx, sy):
        dd = d if dp == 0 else o
        return (dd, lax.rem(x + sx + n_lx, n_lx), lax.rem(y + sy + n_ly, n_ly))

    around = [(dp, sx, sy) for dp in (0, 1) for sx in (-1, 0, 1) for sy in (-1, 0, 1) if (dp, sx, sy) != (0, 0, 0)]

    loads = [
        pltpu.make_async_copy(zn_hbm, zn, ld_sem.at[0]),
        pltpu.make_async_copy(ct_hbm, ct, ld_sem.at[1]),
        pltpu.make_async_copy(it_hbm, fi.at[pl.ds(1, Z)], ld_sem.at[2]),
        pltpu.make_async_copy(st_hbm, st, ld_sem.at[3]),
        pltpu.make_async_copy(rhs_hbm, rh, ld_sem.at[4]),
    ]
    loads.append(pltpu.make_async_copy(mat_hbm, mat, ld_sem.at[5]))
    for item in loads:
        item.start()

    lane = lax.broadcasted_iota(jnp.int32, (8, 128), 1)
    row = lax.broadcasted_iota(jnp.int32, (8, 128), 0)
    zero = jnp.zeros((8, 128), F32)

    rxc[...] = jnp.zeros_like(rxc)
    rcc[...] = jnp.zeros_like(rcc)
    cd[pl.ds(17 * d, 1)] = jnp.zeros((1, 8, 128), F32)
    fi[pl.ds(17 * d, 1)] = jnp.zeros((1, 4, 8, 128), F32)
    cf[pl.ds(17 * d, 1)] = jnp.zeros((1, 4, 8, 128), F32)
    rxi[...] = jnp.zeros_like(rxi)
    rxd[...] = jnp.zeros_like(rxd)
    rci[...] = jnp.zeros_like(rci)
    rcd[...] = jnp.zeros_like(rcd)

    barrier = pltpu.get_barrier_semaphore()
    for place in around:
        pl.semaphore_signal(barrier, inc=1, device_id=near(*place), device_id_type=MESH)

    loads[5].wait()
    for kind in range(2):
        for n, (i, j) in enumerate(SYM):
            line = jnp.concatenate([mat[kind, i, pl.ds(j, 1), :], jnp.zeros((1, 120), F32)], axis=1)
            tab[kind * 10 + n] = pltpu.roll(jnp.broadcast_to(line, (8, 128)), 1, 1)

    loads[0].wait()
    loads[1].wait()
    count = ct[...]
    for z in range(Z):
        cd[z + 1] = jnp.where(z + Z * d < count, zn[z] + 1, 0).astype(F32)

    def pack_columns(ref, comps, first):
        total = zero
        for c in range(comps):
            acc = zero
            for z in range(Z):
                at = 32 * c + 2 * z
                v = ref[first + z, c] if comps > 1 else ref[first + z]
                v = pltpu.roll(v, at + 1, 1)
                acc = jnp.where((lane == at) | (lane == at + 1), v, acc)
            total = total + acc
        return total

    pk[0] = pack_columns(cd, 1, 1)
    for side in range(2):
        sxc[side] = cd[pl.ds(1, Z), 7 * side, :]

    loads[2].wait()
    pk[1] = pack_columns(fi, 4, 1)
    for c in range(4):
        for side in range(2):
            sxi[side, c] = fi[pl.ds(1, Z), c, 7 * side, :]

    pl.semaphore_wait(barrier, len(around))

    face = 15 * o
    far = 17 * d

    def copy(src, dst, n, who):
        return pltpu.make_async_remote_copy(
            src_ref=src, dst_ref=dst, send_sem=send.at[n], recv_sem=recv.at[n], device_id=who, device_id_type=MESH
        )

    def halo_copies(base, plane, pack, srow, rrow, ry, rc, comps):
        out = []

        def add(src, dst, who):
            out.append(copy(src, dst, base + len(out), who))

        for dp in (1, 0):
            for sx in (-1, 1):
                for sy in (-1, 1):
                    r = 7 if sx == 1 else 0
                    add(
                        pack.at[pl.ds(r, 1)],
                        rc.at[dp, 1 if sy == -1 else 0, pl.ds(r, 1)],
                        near(dp, sx, sy),
                    )
            for sy in (-1, 1):
                add(pack, ry.at[dp, 1 if sy == -1 else 0], near(dp, 0, sy))
            for sx in (-1, 1):
                s_side = 0 if sx == -1 else 1
                for c in range(comps):
                    src = srow.at[s_side, c] if comps > 1 else srow.at[s_side]
                    dst = rrow.at[1 - s_side, c] if comps > 1 else rrow.at[1 - s_side]
                    if dp == 1:
                        add(src.at[pl.ds(face, 1)], dst.at[pl.ds(far, 1)], near(1, sx, 0))
                    else:
                        add(src, dst.at[pl.ds(1, Z)], near(0, sx, 0))
        add(plane.at[pl.ds(face + 1, 1)], plane.at[pl.ds(far, 1)], near(1, 0, 0))
        return out

    code_copies = halo_copies(0, cd, pk.at[0], sxc, rxc, ryc, rcc, 1)
    for item in code_copies:
        item.start()
    field_copies = halo_copies(len(code_copies), fi, pk.at[1], sxi, rxi, ryi, rci, 4)
    for item in field_copies:
        item.start()
    used = len(code_copies) + len(field_copies)

    def lookup(code, kind):
        shape = code.shape
        index = code.astype(jnp.int32)
        out = []
        for n in range(10):
            parts = []
            for r in range(shape[0] // 8):
                parts.append(jnp.take_along_axis(tab[kind * 10 + n], index[8 * r : 8 * r + 8], axis=1))
            out.append(parts[0] if len(parts) == 1 else jnp.concatenate(parts, axis=0))
        return out

    def plane_coefficients(q):
        code = cd[q]
        values = lookup(code, 0)
        for n in range(10):
            kl[q, n] = values[n]
        kl[q, 10] = (code > 0).astype(F32)
        for n, v in enumerate(lookup(code, 1)):
            mv[q, n] = v

    def own_plane(z, _):
        plane_coefficients(z + 1)
        return 0

    lax.fori_loop(0, Z, own_plane, 0)
    for n in range(11):
        kl[17 * d, n] = zero
    for n in range(10):
        mv[17 * d, n] = zero

    def field_plane(src, q):
        act = kl[q, 10]
        v = [src[q, c] for c in range(4)]
        k = [kl[q, n] for n in range(10)]
        prod = sym_apply(k, v)
        for c in range(4):
            gf[q, c] = act * v[c]
            gf[q, 4 + c] = prod[c]

    def own_field(z, _):
        field_plane(fi, z + 1)
        return 0

    lax.fori_loop(0, Z, own_field, 0)

    for item in code_copies:
        item.wait_recv()

    near_plane = 17 * o
    plane_coefficients(near_plane)

    odd = (lane & 1) == 1
    other_at = 32 + 94 * d
    own_lane = lane < 32
    other_lane = (lane == other_at) | (lane == other_at + 1)

    def merge(ref, c):
        mine = jnp.where(odd, ref[0, 1], ref[0, 0])
        theirs = jnp.where(odd, ref[1, 1], ref[1, 0])
        if c > 0:
            mine = pltpu.roll(mine, 128 - 32 * c, 1)
        theirs = pltpu.roll(theirs, lax.rem(160 + 64 * d - 32 * c, 128), 1)
        return jnp.where(other_lane, theirs, jnp.where(own_lane, mine, 0.0))

    left_out = jnp.where(y == 0, 0, 1)
    right_out = jnp.where(y == n_ly - 1, 0, 1)
    below_out = jnp.where(x == 0, 0, 1)
    above_out = jnp.where(x == n_lx - 1, 0, 1)
    side_in = jnp.where(odd, right_out, left_out).astype(F32)
    corner_in = jnp.where(row == 7, below_out, above_out).astype(F32) * side_in
    for part, ref in ((0, ryc), (1, rcc)):
        code = merge(ref, 0) * (side_in if part == 0 else corner_in)
        values = lookup(code, 0)
        for n in range(10):
            kly[n, part] = values[n]
        kly[10, part] = (code > 0).astype(F32)
    for side in range(2):
        inside = (below_out if side == 0 else above_out).astype(F32)
        code = rxc[side] * inside
        values = lookup(code, 0)
        for n in range(10):
            klx[n, side] = values[n]
        klx[10, side] = (code > 0).astype(F32)

    def z_mix(v):
        return v + 0.5 * (pltpu.roll(v, 2, 1) + pltpu.roll(v, 126, 1))

    def around_rows(n, u, yc):
        u, yc = z_mix(u), z_mix(yc)
        hi = pltpu.roll(jnp.where(row == 7, yc, u), 1, 0)
        lo = pltpu.roll(jnp.where(row == 0, yc, u), 7, 0)
        yt[n] = u + 0.5 * (hi + lo)

    def row_sums(ref, n):
        for side in range(2):
            xt[n, side] = ref[n, side, pl.ds(1, Z), :] + 0.5 * (
                ref[n, side, pl.ds(0, Z), :] + ref[n, side, pl.ds(2, Z), :]
            )

    for n in range(11):
        around_rows(n, kly[n, 0], kly[n, 1])
        row_sums(klx, n)

    def lateral(ref, z, fields):
        mid = ref[z + 1, pl.ds(0, fields)] + 0.5 * (ref[z, pl.ds(0, fields)] + ref[z + 2, pl.ds(0, fields)])
        out = []
        for n in range(fields):
            v = mid[n]
            hi = jnp.where(row == 0, xt[n, 0, pl.ds(z, 1), :], pltpu.roll(v, 1, 0))
            lo = jnp.where(row == 7, xt[n, 1, pl.ds(z, 1), :], pltpu.roll(v, 7, 0))
            r = 0.5 * (hi + lo)
            s = v + r
            edge = pltpu.roll(yt[n], 127 - 2 * z, 1)
            left = pltpu.roll(jnp.where(lane == 127, edge, s), 1, 1)
            right = pltpu.roll(jnp.where(lane == 0, edge, s), 127, 1)
            out.append(r + 0.5 * (left + right))
        return out

    def couple(j):
        half = 0.5 * kl[j, 10] * kl[j + 1, 10]
        for n in range(10):
            mv[j, n] = half * (mv[j, n] + mv[j + 1, n])

    def couple_step(j, _):
        couple(j)
        return 0

    lax.fori_loop(0, 17, couple_step, 0)

    loads[3].wait()

    def block_step(z, _):
        sums = lateral(kl, z, 11)
        act = kl[z + 1, 10]
        half = 0.5 * act
        store = jnp.where(act > 0, st[z], 1.0)
        for n, (i, j) in enumerate(SYM):
            value = half * (kl[z + 1, n] * sums[10] + sums[n]) + (mv[z, n] + mv[z + 1, n])
            if i == j:
                value = value + store
                sc[z, i] = 1.0 / value
            lk[z, n] = value
        return 0

    lax.fori_loop(0, Z, block_step, 0)

    def place(t):
        return jnp.where(d == 0, t, 15 - t)

    def factor(s, scale, pair):
        xs = sym_inverse(s, scale)
        g = [[None] * 4 for _ in range(4)]
        for j in range(4):
            column = sym_apply(xs, [pair[AT[k, j]] for k in range(4)])
            for i in range(4):
                g[i][j] = column[i]
        nxt = []
        for i, j in SYM:
            a = pair[AT[i, 0]] * g[0][j] + pair[AT[i, 1]] * g[1][j]
            b = pair[AT[i, 2]] * g[2][j] + pair[AT[i, 3]] * g[3][j]
            nxt.append(a + b)
        return xs, g, nxt

    def chain(t, carry):
        z = place(t)
        s = [lk[z, n] - carry[n] for n in range(10)]
        xs, g, nxt = factor(s, [sc[z, i] for i in range(4)], [mv[z + o, n] for n in range(10)])
        for n in range(10):
            inv[z, n] = xs[n]
        for i in range(4):
            for j in range(4):
                gain[z, 4 * i + j] = g[i][j]
        for n in range(10):
            cu[n] = s[n]
        return tuple(nxt)

    last = lax.fori_loop(0, Z, chain, (zero,) * 10)
    for n in range(10):
        ifm_s[n] = last[n]
    matrix_copy = copy(ifm_s, ifm_r, used, near(1, 0, 0))
    matrix_copy.start()

    for item in field_copies:
        item.wait_recv()
    loads[4].wait()

    def halo_fields(rx, ry, rc):
        for part, ref in ((0, ry), (1, rc)):
            v = [merge(ref, c) for c in range(4)]
            prod = sym_apply([kly[n, part] for n in range(10)], v)
            for c in range(4):
                gt[c, part] = kly[10, part] * v[c]
                gt[4 + c, part] = prod[c]
        for side in range(2):
            v = [rx[side, c] for c in range(4)]
            prod = sym_apply([klx[n, side] for n in range(10)], v)
            for c in range(4):
                gx[c, side] = klx[10, side] * v[c]
                gx[4 + c, side] = prod[c]
        for n in range(8):
            around_rows(n, gt[n, 0], gt[n, 1])
            row_sums(gx, n)

    halo_fields(rxi, ryi, rci)
    field_plane(fi, 17 * d)
    field_plane(fi, near_plane)

    def neighbour_part(z):
        sums = lateral(gf, z, 8)
        half = 0.5 * kl[z + 1, 10]
        prod = sym_apply([kl[z + 1, n] for n in range(10)], sums[:4])
        return [half * (prod[c] + sums[4 + c]) for c in range(4)]

    def right_step(z, _):
        part = neighbour_part(z)
        on = kl[z + 1, 10] > 0
        for c in range(4):
            bv[z, c] = jnp.where(on, rh[z, c] + part[c], fi[z + 1, c])
        return 0

    lax.fori_loop(0, Z, right_step, 0)

    def forward(t, carry):
        z = place(t)
        v = [bv[z, c] + carry[c] for c in range(4)]
        r = sym_apply([inv[z, n] for n in range(10)], v)
        for c in range(4):
            rest[z, c] = r[c]
        g = [gain[z, n] for n in range(16)]
        out = []
        for i in range(4):
            out.append((g[i] * v[0] + g[4 + i] * v[1]) + (g[8 + i] * v[2] + g[12 + i] * v[3]))
        for c in range(4):
            bv[z, c] = v[c]
        return tuple(out)

    carried = lax.fori_loop(0, Z, forward, (zero,) * 4)
    for c in range(4):
        ifv_s[c] = carried[c]
    vector_copy = copy(ifv_s, ifv_r, used + 1, near(1, 0, 0))
    vector_copy.start()

    matrix_copy.wait_recv()
    end = place(15)
    closing = sym_inverse([cu[n] - ifm_r[n] for n in range(10)], [sc[end, i] for i in range(4)])
    vector_copy.wait_recv()
    u = sym_apply(closing, [bv[end, c] + ifv_r[c] for c in range(4)])

    def settle(z, values):
        for c in range(4):
            up[z, c] = values[c]
            cf[z + 1, c] = values[c] - fi[z + 1, c]

    settle(end, u)

    def backward(k, carry):
        z = place(14 - k)
        out = []
        for i in range(4):
            a = gain[z, 4 * i] * carry[0] + gain[z, 4 * i + 1] * carry[1]
            b = gain[z, 4 * i + 2] * carry[2] + gain[z, 4 * i + 3] * carry[3]
            out.append(rest[z, i] + (a + b))
        settle(z, out)
        return tuple(out)

    lax.fori_loop(0, Z - 1, backward, tuple(u))
    up_copy = pltpu.make_async_copy(up, up_hbm, out_sem.at[0])
    up_copy.start()

    pk[2] = pack_columns(cf, 4, 1)
    for c in range(4):
        for side in range(2):
            sxd[side, c] = cf[pl.ds(1, Z), c, 7 * side, :]
    change_copies = halo_copies(used + 2, cf, pk.at[2], sxd, rxd, ryd, rcd, 4)
    for item in change_copies:
        item.start()

    def own_change(z, _):
        field_plane(cf, z + 1)
        return 0

    lax.fori_loop(0, Z, own_change, 0)
    for item in change_copies:
        item.wait_recv()
    halo_fields(rxd, ryd, rcd)
    field_plane(cf, 17 * d)
    field_plane(cf, near_plane)

    def smooth_step(t, _):
        z = place(15 - t)
        part = neighbour_part(z)
        for c in range(4):
            sm[z, c] = part[c]
        return 0

    smooth_step(0, 0)
    top_copy = copy(sm.at[face], sm_r, used + 2 + len(change_copies), near(1, 0, 0))
    top_copy.start()
    lax.fori_loop(1, Z, smooth_step, 0)
    top_copy.wait_recv()

    from_below = jnp.where(d == 0, 0.0, 1.0)
    for k in range(Z // 2):
        for c in range(4):
            before = sm_r[c] * from_below if k == 0 else sm[2 * k - 1, c]
            cu[4 * k + c] = 0.5 * before + sm[2 * k, c] + 0.5 * sm[2 * k + 1, c]
    coarse_copies = []
    for k in range(Z // 2):
        coarse_copies.append(pltpu.make_async_copy(cu.at[pl.ds(4 * k, 4)], co_hbm.at[k], out_sem.at[1 + k]))
        coarse_copies[-1].start()
    for item in coarse_copies:
        item.wait()
    up_copy.wait()
    for item in code_copies + field_copies + [matrix_copy, vector_copy] + change_copies + [top_copy]:
        item.wait_send()


def local(sizes, iterate, right_side, storage, zones, counts, materials):
    V = pltpu.VMEM
    any_spec = pl.BlockSpec(memory_space=pl.ANY)
    blk = (8, 128)
    messages = 25 + 2 * 37 + 3
    shapes = [
        V((2, 4, 4, 8), F32),
        V((18, 4) + blk, F32),
        V((Z, 4) + blk, F32),
        V((Z,) + blk, F32),
        V((Z,) + blk, jnp.int32),
        V(blk, jnp.int32),
        V((20,) + blk, F32),
        V((18,) + blk, F32),
        V((18, 11) + blk, F32),
        V((18, 10) + blk, F32),
        V((Z, 10) + blk, F32),
        V((18, 8) + blk, F32),
        V((18, 4) + blk, F32),
        V((Z, 4) + blk, F32),
        V((Z, 4) + blk, F32),
        V((32,) + blk, F32),
        V((Z, 10) + blk, F32),
        V((Z, 16) + blk, F32),
        V((Z, 4) + blk, F32),
        V((Z, 4) + blk, F32),
        V((Z, 4) + blk, F32),
        V((3,) + blk, F32),
        V((2, Z, 128), F32),
        V((2, 4, Z, 128), F32),
        V((2, 4, Z, 128), F32),
        V((2, 24, 128), F32),
        V((2, 4, 24, 128), F32),
        V((2, 4, 24, 128), F32),
        V((2, 2) + blk, F32),
        V((2, 2) + blk, F32),
        V((2, 2) + blk, F32),
        V((2, 2) + blk, F32),
        V((2, 2) + blk, F32),
        V((2, 2) + blk, F32),
        V((11, 2, 24, 128), F32),
        V((11, 2) + blk, F32),
        V((8, 2, 24, 128), F32),
        V((8, 2) + blk, F32),
        V((11, 2, Z, 128), F32),
        V((11,) + blk, F32),
        V((10,) + blk, F32),
        V((10,) + blk, F32),
        V((4,) + blk, F32),
        V((4,) + blk, F32),
        V((4,) + blk, F32),
        pltpu.SemaphoreType.DMA((6,)),
        pltpu.SemaphoreType.DMA((9,)),
        pltpu.SemaphoreType.DMA((messages,)),
        pltpu.SemaphoreType.DMA((messages,)),
    ]
    return pl.pallas_call(
        functools.partial(kernel, sizes),
        out_shape=(
            jax.ShapeDtypeStruct((Z, 4) + blk, F32),
            jax.ShapeDtypeStruct((Z // 2, 4) + blk, F32),
        ),
        in_specs=[any_spec] * 6,
        out_specs=(any_spec, any_spec),
        scratch_shapes=shapes,
        compiler_params=pltpu.CompilerParams(collective_id=0, has_side_effects=True),
        name="zline",
    )(iterate, right_side, storage, zones, counts, jnp.transpose(materials, (0, 2, 3, 1)))


def solution(mesh):
    placed = (
        P("depth", None, "lx", "ly"),
        P("depth", None, "lx", "ly"),
        P("depth", "lx", "ly"),
        P("depth", "lx", "ly"),
        P("lx", "ly"),
        P(),
    )
    sizes = (mesh.shape["lx"], mesh.shape["ly"])
    return jax.shard_map(
        functools.partial(local, sizes),
        mesh=mesh,
        in_specs=placed,
        out_specs=(P("depth", None, "lx", "ly"), P("depth", None, "lx", "ly")),
        check_vma=False,
    )
```

time: 182 us -> 39.1 us (0.21)
  the two profiles are of different devices: /device:TPU:153 before, /device:TPU:1 now
where the time goes in v1:
time: 39.1 us; the launch traced here: 38.9 us
  Pallas kernels  35.9 us (92%)
  local copies, waits for them, and re-layouts  2.37 us (6%)
  between operations  0.65 us (2%)
    pallas_call x1, Pallas kernels, local(): pl.pallas_call(functools.partial(kernel, sizes), out_shape=(jax.ShapeDtyp...  35.9 us
    unnamed x4, local copies, waits for them, and re-layouts  2.37 us

profile of v1, /device:TPU:1, one launch (start us, length us, event | category | flops | bytes accessed | tf_op | source)
XLA Modules:
  0.0 38.9 jit_solution(415514534741584917)
XLA Ops:
  0.6 35.9 %zline.1 = (f32[16,4,8,128]{3,2,1,0:T(8,128)}, f32[8,4,8,128]{3,2,1,0:T(8,128)}) custom-call(f32[16,4,8,128]{3,2,1,0:T(8,128)} %it_hbm.1, f32[16,4,8,128]{3,2,1,0:T(8,128)} %rhs_hbm.1, f32[16,8,128]{2,1,0:T(8,128)} %st_hbm.1, s32[16,8,128]{2,1,0:T(8,128)} %zn_hbm.1, s32[8,128]{1,0:T(8,128)} %ct_hbm.1, f32[2,4,4,8]{3,2,1,0:T(4,128)} %bitcast.1), custom_call_target="tpu_custom_call" | custom-call | tf_op jit(solution)/shard_map/zline/pallas_call | solution.py:558
  36.5 0.0 copy-start
  36.6 1.7 %copy.10 = f32[16,4,8,128]{3,2,1,0:T(8,128)} copy(f32[16,4,8,128]{3,2,1,0:T(8,128)} %get-tuple-element.4) | data formatting | bytes 524288
  38.3 0.0 copy-done
  38.3 0.7 %copy.11 = f32[8,4,8,128]{3,2,1,0:T(8,128)} copy(f32[8,4,8,128]{3,2,1,0:T(8,128)S(1)} %copy-done) | data formatting | bytes 262144
Async XLA Ops:
  36.5 1.7 %copy-start = (f32[8,4,8,128]{3,2,1,0:T(8,128)S(1)}, f32[8,4,8,128]{3,2,1,0:T(8,128)}, u32[]{:S(2)}) copy-start(f32[8,4,8,128]{3,2,1,0:T(8,128)} %get-tuple-element.5) | copy-start | bytes 393220

commit v2 on v1

--- a/solution.py
+++ b/solution.py
@@ -15,6 +15,11 @@
 for _n, (_i, _j) in enumerate(SYM):
     AT[_i, _j] = _n
     AT[_j, _i] = _n
+
+
+def face_rows(ref, comps, c, side):
+    flat = ref.reshape(18 * comps * 8, 128)
+    return flat[pl.ds(8 * comps + 8 * c + 7 * side, Z, stride=8 * comps), :]
 
 
 def sym_apply(m, v):
@@ -68,9 +73,21 @@
 
     def near(dp, sx, sy):
         dd = d if dp == 0 else o
-        return (dd, lax.rem(x + sx + n_lx, n_lx), lax.rem(y + sy + n_ly, n_ly))
-
-    around = [(dp, sx, sy) for dp in (0, 1) for sx in (-1, 0, 1) for sy in (-1, 0, 1) if (dp, sx, sy) != (0, 0, 0)]
+        return (dd, x + sx, y + sy)
+
+    def exists(sx, sy):
+        tests = []
+        if sx != 0:
+            tests.append(x > 0 if sx < 0 else x < n_lx - 1)
+        if sy != 0:
+            tests.append(y > 0 if sy < 0 else y < n_ly - 1)
+        if len(tests) == 2:
+            return jnp.logical_and(*tests)
+        return tests[0]
+
+    ways = [(sx, sy) for sx in (-1, 0, 1) for sy in (-1, 0, 1) if (sx, sy) != (0, 0)]
+    span_x = 3 - jnp.where(x == 0, 1, 0) - jnp.where(x == n_lx - 1, 1, 0)
+    span_y = 3 - jnp.where(y == 0, 1, 0) - jnp.where(y == n_ly - 1, 1, 0)
 
     loads = [
         pltpu.make_async_copy(zn_hbm, zn, ld_sem.at[0]),
@@ -87,8 +104,8 @@
     row = lax.broadcasted_iota(jnp.int32, (8, 128), 0)
     zero = jnp.zeros((8, 128), F32)
 
-    rxc[...] = jnp.zeros_like(rxc)
-    rcc[...] = jnp.zeros_like(rcc)
+    for ref in (rxc, rcc, ryc, ryi, ryd):
+        ref[...] = jnp.zeros_like(ref)
     cd[pl.ds(17 * d, 1)] = jnp.zeros((1, 8, 128), F32)
     fi[pl.ds(17 * d, 1)] = jnp.zeros((1, 4, 8, 128), F32)
     cf[pl.ds(17 * d, 1)] = jnp.zeros((1, 4, 8, 128), F32)
@@ -98,8 +115,13 @@
     rcd[...] = jnp.zeros_like(rcd)
 
     barrier = pltpu.get_barrier_semaphore()
-    for place in around:
-        pl.semaphore_signal(barrier, inc=1, device_id=near(*place), device_id_type=MESH)
+    pl.semaphore_signal(barrier, inc=1, device_id=near(1, 0, 0), device_id_type=MESH)
+    for way in ways:
+
+        @pl.when(exists(*way))
+        def _():
+            for dp in (0, 1):
+                pl.semaphore_signal(barrier, inc=1, device_id=near(dp, *way), device_id_type=MESH)
 
     loads[5].wait()
     for kind in range(2):
@@ -127,15 +149,15 @@
 
     pk[0] = pack_columns(cd, 1, 1)
     for side in range(2):
-        sxc[side] = cd[pl.ds(1, Z), 7 * side, :]
+        sxc[side] = face_rows(cd, 1, 0, side)
 
     loads[2].wait()
     pk[1] = pack_columns(fi, 4, 1)
     for c in range(4):
         for side in range(2):
-            sxi[side, c] = fi[pl.ds(1, Z), c, 7 * side, :]
-
-    pl.semaphore_wait(barrier, len(around))
+            sxi[side, c] = face_rows(fi, 4, c, side)
+
+    pl.semaphore_wait(barrier, 2 * span_x * span_y - 1)
 
     face = 15 * o
     far = 17 * d
@@ -145,42 +167,53 @@
             src_ref=src, dst_ref=dst, send_sem=send.at[n], recv_sem=recv.at[n], device_id=who, device_id_type=MESH
         )
 
-    def halo_copies(base, plane, pack, srow, rrow, ry, rc, comps):
-        out = []
-
-        def add(src, dst, who):
-            out.append(copy(src, dst, base + len(out), who))
-
-        for dp in (1, 0):
-            for sx in (-1, 1):
-                for sy in (-1, 1):
-                    r = 7 if sx == 1 else 0
-                    add(
-                        pack.at[pl.ds(r, 1)],
-                        rc.at[dp, 1 if sy == -1 else 0, pl.ds(r, 1)],
-                        near(dp, sx, sy),
-                    )
-            for sy in (-1, 1):
-                add(pack, ry.at[dp, 1 if sy == -1 else 0], near(dp, 0, sy))
-            for sx in (-1, 1):
-                s_side = 0 if sx == -1 else 1
-                for c in range(comps):
-                    src = srow.at[s_side, c] if comps > 1 else srow.at[s_side]
-                    dst = rrow.at[1 - s_side, c] if comps > 1 else rrow.at[1 - s_side]
-                    if dp == 1:
-                        add(src.at[pl.ds(face, 1)], dst.at[pl.ds(far, 1)], near(1, sx, 0))
+    class Halo:
+        def __init__(self, base, plane, pack, srow, rrow, ry, rc, comps):
+            every = (slice(None),) if comps > 1 else ()
+            self.groups = {}
+            for sx, sy in ways:
+                group = []
+                for dp in (1, 0):
+                    n = base + 2 * ways.index((sx, sy)) + dp
+                    side = 1 if sy == -1 else 0
+                    if sx != 0 and sy != 0:
+                        r = 7 if sx == 1 else 0
+                        src, dst = pack.at[pl.ds(r, 1)], rc.at[dp, side, pl.ds(r, 1)]
+                    elif sx == 0:
+                        src, dst = pack, ry.at[dp, side]
                     else:
-                        add(src, dst.at[pl.ds(1, Z)], near(0, sx, 0))
-        add(plane.at[pl.ds(face + 1, 1)], plane.at[pl.ds(far, 1)], near(1, 0, 0))
-        return out
-
-    code_copies = halo_copies(0, cd, pk.at[0], sxc, rxc, ryc, rcc, 1)
-    for item in code_copies:
-        item.start()
-    field_copies = halo_copies(len(code_copies), fi, pk.at[1], sxi, rxi, ryi, rci, 4)
-    for item in field_copies:
-        item.start()
-    used = len(code_copies) + len(field_copies)
+                        s_side = 0 if sx == -1 else 1
+                        src, dst = srow.at[s_side], rrow.at[1 - s_side]
+                        if dp == 1:
+                            src, dst = src.at[every + (pl.ds(face, 1),)], dst.at[every + (pl.ds(far, 1),)]
+                        else:
+                            dst = dst.at[every + (pl.ds(1, Z),)]
+                    group.append(copy(src, dst, n, near(dp, sx, sy)))
+                self.groups[sx, sy] = group
+            self.across = copy(plane.at[pl.ds(face + 1, 1)], plane.at[pl.ds(far, 1)], base + 16, near(1, 0, 0))
+
+        def each(self, act, flip):
+            act(self.across)
+            for (sx, sy), group in self.groups.items():
+
+                @pl.when(exists(flip * sx, flip * sy))
+                def _():
+                    for item in group:
+                        act(item)
+
+        def start(self):
+            self.each(lambda item: item.start(), 1)
+
+        def wait_recv(self):
+            self.each(lambda item: item.wait_recv(), -1)
+
+        def wait_send(self):
+            self.each(lambda item: item.wait_send(), 1)
+
+    code_halo = Halo(0, cd, pk.at[0], sxc, rxc, ryc, rcc, 1)
+    code_halo.start()
+    field_halo = Halo(17, fi, pk.at[1], sxi, rxi, ryi, rci, 4)
+    field_halo.start()
 
     def lookup(code, kind):
         shape = code.shape
@@ -227,8 +260,7 @@
 
     lax.fori_loop(0, Z, own_field, 0)
 
-    for item in code_copies:
-        item.wait_recv()
+    code_halo.wait_recv()
 
     near_plane = 17 * o
     plane_coefficients(near_plane)
@@ -246,21 +278,14 @@
         theirs = pltpu.roll(theirs, lax.rem(160 + 64 * d - 32 * c, 128), 1)
         return jnp.where(other_lane, theirs, jnp.where(own_lane, mine, 0.0))
 
-    left_out = jnp.where(y == 0, 0, 1)
-    right_out = jnp.where(y == n_ly - 1, 0, 1)
-    below_out = jnp.where(x == 0, 0, 1)
-    above_out = jnp.where(x == n_lx - 1, 0, 1)
-    side_in = jnp.where(odd, right_out, left_out).astype(F32)
-    corner_in = jnp.where(row == 7, below_out, above_out).astype(F32) * side_in
     for part, ref in ((0, ryc), (1, rcc)):
-        code = merge(ref, 0) * (side_in if part == 0 else corner_in)
+        code = merge(ref, 0)
         values = lookup(code, 0)
         for n in range(10):
             kly[n, part] = values[n]
         kly[10, part] = (code > 0).astype(F32)
     for side in range(2):
-        inside = (below_out if side == 0 else above_out).astype(F32)
-        code = rxc[side] * inside
+        code = rxc[side]
         values = lookup(code, 0)
         for n in range(10):
             klx[n, side] = values[n]
@@ -361,11 +386,10 @@
     last = lax.fori_loop(0, Z, chain, (zero,) * 10)
     for n in range(10):
         ifm_s[n] = last[n]
-    matrix_copy = copy(ifm_s, ifm_r, used, near(1, 0, 0))
+    matrix_copy = copy(ifm_s, ifm_r, 51, near(1, 0, 0))
     matrix_copy.start()
 
-    for item in field_copies:
-        item.wait_recv()
+    field_halo.wait_recv()
     loads[4].wait()
 
     def halo_fields(rx, ry, rc):
@@ -421,7 +445,7 @@
     carried = lax.fori_loop(0, Z, forward, (zero,) * 4)
     for c in range(4):
         ifv_s[c] = carried[c]
-    vector_copy = copy(ifv_s, ifv_r, used + 1, near(1, 0, 0))
+    vector_copy = copy(ifv_s, ifv_r, 52, near(1, 0, 0))
     vector_copy.start()
 
     matrix_copy.wait_recv()
@@ -454,18 +478,16 @@
     pk[2] = pack_columns(cf, 4, 1)
     for c in range(4):
         for side in range(2):
-            sxd[side, c] = cf[pl.ds(1, Z), c, 7 * side, :]
-    change_copies = halo_copies(used + 2, cf, pk.at[2], sxd, rxd, ryd, rcd, 4)
-    for item in change_copies:
-        item.start()
+            sxd[side, c] = face_rows(cf, 4, c, side)
+    change_halo = Halo(34, cf, pk.at[2], sxd, rxd, ryd, rcd, 4)
+    change_halo.start()
 
     def own_change(z, _):
         field_plane(cf, z + 1)
         return 0
 
     lax.fori_loop(0, Z, own_change, 0)
-    for item in change_copies:
-        item.wait_recv()
+    change_halo.wait_recv()
     halo_fields(rxd, ryd, rcd)
     field_plane(cf, 17 * d)
     field_plane(cf, near_plane)
@@ -478,7 +500,7 @@
         return 0
 
     smooth_step(0, 0)
-    top_copy = copy(sm.at[face], sm_r, used + 2 + len(change_copies), near(1, 0, 0))
+    top_copy = copy(sm.at[face], sm_r, 53, near(1, 0, 0))
     top_copy.start()
     lax.fori_loop(1, Z, smooth_step, 0)
     top_copy.wait_recv()
@@ -495,7 +517,7 @@
     for item in coarse_copies:
         item.wait()
     up_copy.wait()
-    for item in code_copies + field_copies + [matrix_copy, vector_copy] + change_copies + [top_copy]:
+    for item in (code_halo, field_halo, change_halo, matrix_copy, vector_copy, top_copy):
         item.wait_send()
 
 
@@ -503,7 +525,7 @@
     V = pltpu.VMEM
     any_spec = pl.BlockSpec(memory_space=pl.ANY)
     blk = (8, 128)
-    messages = 25 + 2 * 37 + 3
+    messages = 3 * 17 + 3
     shapes = [
         V((2, 4, 4, 8), F32),
         V((18, 4) + blk, F32),

time: 39.1 us -> 31.9 us (0.82)
  the two profiles are of different devices: /device:TPU:1 before, /device:TPU:56 now
where the time goes in v2:
time: 31.9 us; the launch traced here: 31.7 us
  Pallas kernels  28.7 us (90%)
  local copies, waits for them, and re-layouts  2.37 us (7%)
  between operations  0.65 us (2%)
    pallas_call x1, Pallas kernels, local(): pl.pallas_call(functools.partial(kernel, sizes), out_shape=(jax.ShapeDtyp...  28.7 us
    unnamed x4, local copies, waits for them, and re-layouts  2.37 us

profile of v2, /device:TPU:56, one launch (start us, length us, event | category | flops | bytes accessed | tf_op | source)
XLA Modules:
  0.0 31.7 jit_solution(10566810703761438235)
XLA Ops:
  0.6 28.7 %zline.1 = (f32[16,4,8,128]{3,2,1,0:T(8,128)}, f32[8,4,8,128]{3,2,1,0:T(8,128)}) custom-call(f32[16,4,8,128]{3,2,1,0:T(8,128)} %it_hbm.1, f32[16,4,8,128]{3,2,1,0:T(8,128)} %rhs_hbm.1, f32[16,8,128]{2,1,0:T(8,128)} %st_hbm.1, s32[16,8,128]{2,1,0:T(8,128)} %zn_hbm.1, s32[8,128]{1,0:T(8,128)} %ct_hbm.1, f32[2,4,4,8]{3,2,1,0:T(4,128)} %bitcast.1), custom_call_target="tpu_custom_call" | custom-call | tf_op jit(solution)/shard_map/zline/pallas_call | solution.py:580
  29.3 0.0 copy-start
  29.3 1.7 %copy.10 = f32[16,4,8,128]{3,2,1,0:T(8,128)} copy(f32[16,4,8,128]{3,2,1,0:T(8,128)} %get-tuple-element.4) | data formatting | bytes 524288
  31.0 0.0 copy-done
  31.0 0.7 %copy.11 = f32[8,4,8,128]{3,2,1,0:T(8,128)} copy(f32[8,4,8,128]{3,2,1,0:T(8,128)S(1)} %copy-done) | data formatting | bytes 262144
Async XLA Ops:
  29.3 1.7 %copy-start = (f32[8,4,8,128]{3,2,1,0:T(8,128)S(1)}, f32[8,4,8,128]{3,2,1,0:T(8,128)}, u32[]{:S(2)}) copy-start(f32[8,4,8,128]{3,2,1,0:T(8,128)} %get-tuple-element.5) | copy-start | bytes 393220
